TPU v7x, 256 devices: a whole 4x4x8 slice. The times are simulated.
256 devices in a mesh: tm: 32 (over x, y, core), row: 8 (over z).
Axes of the slice: x: 4, y: 4, z: 8, core: 2. Of those that a mesh axis runs over, the one named last changes fastest.
Arguments:
- frames_in: bfloat16 [64, 32, 64, 256], P('tm', 'row'), may hold values from -6 to 6
- cotangent: bfloat16 [64, 32, 64, 256], P('tm', 'row'), may hold values from -6 to 6
- kernel: bfloat16 [9, 256, 256], replicated, may hold values from -0.125 to 0.125
- readout: bfloat16 [256, 256], replicated, may hold values from -0.375 to 0.375
- feedthrough: float32 [256], replicated, may hold values from 0.5 to 1.5
- decay_rate: float32 [64, 256], P('tm'), may hold values from 0.05 to 1, as said below
- start_state: float32 [32, 64, 256], P('row'), may hold values from -6 to 6
Outputs:
- grad_frames: bfloat16 [64, 32, 64, 256], P('tm', 'row')
- grad_kernel: float32 [9, 256, 256], P(None, 'row')
- grad_readout: float32 [256, 256], P(None, 'row')
Inputs may be any that keep to these rules, and one draw needn't show every extreme that they name: `decay_rate`: every entry lies strictly between 0 and 1.
All inputs are finite; a program needn't handle non-finite values.
Results may differ from a plain program's by a relative error of at most 0.015.
Values may be sent and summed in bfloat16 or wider, within the bound.
No kernel may reach another device: no remote copies, remote signals or barrier semaphores. Data moves between devices by JAX's collectives and lax.ppermute only.
A program may use at most 64 MiB of HBM per device.

v0:
```python
import math
import jax
import jax.numpy as jnp
from jax import lax
from jax.sharding import PartitionSpec as P

SQRT_TWO_PI = 0.7978845608
CUBIC = 0.044715


def extended(cells, sides, width):
    for axis, dim in sides:
        count = lax.axis_size(axis)
        ends = count - 1
        head = lax.slice_in_dim(cells, 0, width, axis=dim)
        tail = lax.slice_in_dim(cells, cells.shape[dim] - width, cells.shape[dim], axis=dim)
        cells = jnp.concatenate(
            [
                lax.ppermute(tail, axis, [(i, (i + 1) % count) for i in range(ends)]),
                cells,
                lax.ppermute(head, axis, [((i + 1) % count, i) for i in range(ends)]),
            ],
            axis=dim,
        )
    return cells


def carried_in(value, axis, join, neutral, backward):
    count, mine = (lax.axis_size(axis), lax.axis_index(axis))
    pieces = jax.tree.map(lambda part: lax.all_gather(part, axis), value)
    if backward:
        pieces = jax.tree.map(lambda part: part[::-1], pieces)
        mine = count - 1 - mine
    subtotal = jax.tree.map(
        lambda part, zero: jnp.full_like(part, 0) + jnp.asarray(zero, part.dtype), value, neutral
    )

    def turn(position, subtotal):
        longer = join(subtotal, jax.tree.map(lambda part: part[position], pieces))
        return jax.tree.map(lambda new, old: jnp.where(position < mine, new, old), longer, subtotal)

    return lax.fori_loop(0, count - 1, turn, subtotal)


def gelu_slope(mixture):
    inside = SQRT_TWO_PI * (mixture + CUBIC * mixture * mixture * mixture)
    tangent = jnp.tanh(inside)
    return 0.5 * (1.0 + tangent) + 0.5 * mixture * (1.0 - tangent * tangent) * SQRT_TWO_PI * (
        1.0 + 3.0 * CUBIC * mixture * mixture
    )


def block_taps(padded, band_rows, grid_width, flipped):
    pieces = []
    for vertical in range(3):
        for lateral in range(3):
            from_top = 2 - vertical if flipped else vertical
            from_left = 2 - lateral if flipped else lateral
            pieces.append(
                padded[:, from_top : from_top + band_rows, from_left : from_left + grid_width, :]
            )
    return jnp.stack(pieces, axis=3)


def compose(earlier, later):
    return (later[0] * earlier[0], later[0] * earlier[1] + later[1])


def local(frames_in, cotangent, kernel, readout, feedthrough, decay_rate, start_state):
    frames_here, band_rows, grid_width, channels = frames_in.shape
    state_width = kernel.shape[2]
    cell_count = frames_here * band_rows * grid_width
    rimmed = extended(frames_in, (("row", 1),), 1)
    padded = jnp.pad(rimmed, ((0, 0), (0, 0), (1, 1), (0, 0)))
    input_taps = block_taps(padded, band_rows, grid_width, False).reshape(cell_count, 9 * channels)
    driven = jnp.dot(
        input_taps, kernel.reshape(9 * channels, state_width), preferred_element_type=jnp.float32
    )
    driven = driven.reshape(frames_here, band_rows, grid_width, state_width)
    gain_all = jnp.sqrt(1.0 - decay_rate * decay_rate)
    leader = (lax.axis_index("tm") == 0).astype(jnp.float32)

    def advance(carried, inputs):
        driven_now, rate_now, gain_now = inputs
        carried = rate_now * carried + gain_now * driven_now
        return (carried, carried)

    _, local_states = lax.scan(advance, start_state * leader, (driven, decay_rate, gain_all))
    through = jnp.cumprod(decay_rate, axis=0)
    identity = (
        jnp.ones((state_width,), jnp.float32),
        jnp.zeros((band_rows, grid_width, state_width), jnp.float32),
    )
    _, entering = carried_in((through[-1], local_states[-1]), "tm", compose, identity, False)
    states = local_states + through[:, None, None, :] * entering[None]
    state_bf = states.astype(jnp.bfloat16).reshape(cell_count, state_width)
    mixture = jnp.dot(state_bf, readout, preferred_element_type=jnp.float32)
    slope_bf = (
        cotangent.reshape(cell_count, channels).astype(jnp.float32) * gelu_slope(mixture)
    ).astype(jnp.bfloat16)
    pulled = lax.dot_general(
        slope_bf, readout, (((1,), (1,)), ((), ())), preferred_element_type=jnp.float32
    )
    pulled = pulled.reshape(frames_here, band_rows, grid_width, state_width)
    later_rate = jnp.concatenate([decay_rate[1:], jnp.ones((1, state_width), jnp.float32)], axis=0)

    def retreat(carried, inputs):
        pulled_now, rate_next = inputs
        carried = pulled_now + rate_next * carried
        return (carried, carried)

    _, local_adjoint = lax.scan(
        retreat,
        jnp.zeros((band_rows, grid_width, state_width), jnp.float32),
        (pulled, later_rate),
        reverse=True,
    )
    remaining = jnp.flip(jnp.cumprod(jnp.flip(later_rate, 0), axis=0), 0)
    _, arriving = carried_in(
        (through[-1], decay_rate[0][None, None, :] * local_adjoint[0]),
        "tm",
        compose,
        identity,
        True,
    )
    adjoint = local_adjoint + remaining[:, None, None, :] * arriving[None]
    grad_drive = (gain_all[:, None, None, :] * adjoint).astype(jnp.bfloat16)
    rim_adjoint = extended(grad_drive, (("row", 1),), 1)
    padded_drive = jnp.pad(rim_adjoint, ((0, 0), (0, 0), (1, 1), (0, 0)))
    output_taps = block_taps(padded_drive, band_rows, grid_width, True).reshape(
        cell_count, 9, state_width
    )
    spread = lax.dot_general(
        output_taps, kernel, (((1, 2), (0, 2)), ((), ())), preferred_element_type=jnp.float32
    )
    spread = spread.reshape(frames_here, band_rows, grid_width, channels)
    grad_frames = (spread + feedthrough * cotangent.astype(jnp.float32)).astype(jnp.bfloat16)
    kernel_term = lax.dot_general(
        input_taps,
        grad_drive.reshape(cell_count, state_width),
        (((0,), (0,)), ((), ())),
        preferred_element_type=jnp.float32,
    ).reshape(9, channels, state_width)
    readout_term = lax.dot_general(
        state_bf, slope_bf, (((0,), (0,)), ((), ())), preferred_element_type=jnp.float32
    )
    band_count = lax.axis_size("row")
    scaling = 1.0 / math.sqrt(cell_count * lax.axis_size("tm") * band_count)
    share_width = channels // band_count
    kernel_all, readout_all = lax.psum((kernel_term, readout_term), ("tm", "row"))
    offset_start = lax.axis_index("row") * share_width
    kernel_part = lax.dynamic_slice_in_dim(kernel_all, offset_start, share_width, 1)
    readout_part = lax.dynamic_slice_in_dim(readout_all, offset_start, share_width, 1)
    return (grad_frames, kernel_part * scaling, readout_part * scaling)


def solution(mesh):
    placed = (
        P("tm", "row", None, None),
        P("tm", "row", None, None),
        P(),
        P(),
        P(),
        P("tm", None),
        P("row", None, None),
    )
    return jax.shard_map(
        local,
        mesh=mesh,
        in_specs=placed,
        out_specs=(P("tm", "row", None, None), P(None, "row", None), P(None, "row")),
        check_vma=False,
    )
```

profile of v0, /device:TPU:2, one launch (start us, length us, event | category | flops | bytes accessed | tf_op | source)
XLA Modules:
  0.0 510.4 jit_solution(2149309793703916554)
XLA Ops:
  8.2 3.8 collective-permute-start
  12.1 1.3 collective-permute-start.1
  15.1 3.2 collective-permute-done.1
  23.3 24.2 %all-gather = f32[32,1,256]{2,1,0:T(1,128)S(1)} all-gather(f32[1,1,256]{2,1,0:T(1,128)S(1)} %slice_bitcast_fusion.12), channel_id=1, replica_groups=mesh['tm'=32,'row'=8] {'tm'}, dimensions={0}, use_global_device_ids=true | all-gather | bytes 33792 | tf_op jit(solution)/shard_map/all_gather | solution.py:30
  47.6 36.4 %all-gather.4.cloned.1.call-done = f32[32,4,64,256]{3,2,1,0:T(8,128)} async-done(((f32[1,4,64,256]{3,2,1,0:T(8,128)}), f32[32,4,64,256]{3,2,1,0:T(8,128)}) %all-gather.4.cloned.1.call-update) | async-done | bytes 8388624 | tf_op jit(solution)/shard_map/all_gather | solution.py:30
  84.0 36.9 %while.58 = (s32[]{:T(128)}, f32[4,64,256]{2,1,0:T(8,128)S(1)}, s32[]{:T(128)}, f32[32,256]{1,0:T(8,128)S(1)}, f32[32,4,64,256]{3,2,1,0:T(8,128)}, /*index=5*/s32[]{:T(128)}, s32[]{:T(128)}) while((s32[]{:T(128)}, f32[4,64,256]{2,1,0:T(8,128)S(1)}, s32[]{:T(128)}, f32[32,256]{1,0:T(8,128)S(1)}, f32[32,4,64,256]{3,2,1,0:T(8,128)}, ...), condition=%wide.region_4.5_spmd.clone, body=%wide.region_3.4_spmd.clone.sunk | while | flops 262148 | bytes 789609 | solution.py:42
  84.0 1.2 fusion.59
  85.2 1.1 fusion.59
  86.4 1.1 fusion.59
  87.6 1.1 fusion.59
  88.8 1.1 fusion.59
  123.2 3.3 copy.51
  126.5 2.8 copy.57
  129.3 4.3 copy.52
  134.5 45.9 %all-gather.6.cloned.1.call-done = f32[32,4,64,256]{3,2,1,0:T(8,128)} async-done(((f32[1,4,64,256]{3,2,1,0:T(8,128)}), f32[32,4,64,256]{3,2,1,0:T(8,128)}) %all-gather.6.cloned.1.call-update) | async-done | bytes 8388624 | tf_op jit(solution)/shard_map/all_gather | solution.py:30
  180.4 7.7 %rev.16 = f32[32,4,64,256]{3,2,1,0:T(8,128)} reverse(f32[32,4,64,256]{3,2,1,0:T(8,128)} %all-gather.6.cloned.1.call-done), dimensions={0} | reverse | bytes 16777216 | tf_op jit(solution)/shard_map/rev | solution.py:32
  188.1 36.8 %while.60 = (s32[]{:T(128)}, f32[4,64,256]{2,1,0:T(8,128)S(1)}, s32[]{:T(128)}, f32[32,256]{1,0:T(8,128)S(1)}, f32[32,4,64,256]{3,2,1,0:T(8,128)}, /*index=5*/s32[]{:T(128)}, s32[]{:T(128)}) while((s32[]{:T(128)}, f32[4,64,256]{2,1,0:T(8,128)S(1)}, s32[]{:T(128)}, f32[32,256]{1,0:T(8,128)S(1)}, f32[32,4,64,256]{3,2,1,0:T(8,128)}, ...), condition=%wide.region_9.10_spmd.clone, body=%wide.region_8.9_spmd.clone.sunk | while | flops 262148 | bytes 789609 | solution.py:42
  225.1 3.5 collective-permute-start.2
  228.6 1.3 collective-permute-start.3
  229.9 3.9 fusion.45
  235.9 1.5 fusion.4
  237.4 263.4 %all-reduce.6.cloned.1.call-done = (f32[9,256,256]{2,1,0:T(8,128)}, f32[256,256]{0,1:T(8,128)}) async-done(((f32[9,256,256]{2,1,0:T(8,128)}, f32[256,256]{0,1:T(8,128)}), (f32[9,256,256]{2,1,0:T(8,128)}, f32[256,256]{0,1:T(8,128)})) %all-reduce.6.cloned.1.call-update) | async-done | bytes 2621456 | tf_op jit(solution)/shard_map/psum | solution.py:150
  500.8 1.7 dynamic-slice_multiply_fusion
  502.5 1.4 dynamic-slice_multiply_fusion.1
  (200 shorter events, 79.6 us)
Async XLA Ops:
  7.2 13.5 %copy-start = (bf16[9,256,256]{2,1,0:T(8,128)(2,1)S(1)}, bf16[9,256,256]{2,1,0:T(8,128)(2,1)}, u32[]{:S(2)}) copy-start(bf16[9,256,256]{2,1,0:T(8,128)(2,1)} %param.17) | copy-start | bytes 3538948
  7.2 13.2 %copy-start.1 = (bf16[2,4,64,256]{3,2,1,0:T(8,128)(2,1)S(1)}, bf16[2,4,64,256]{3,2,1,0:T(8,128)(2,1)}, u32[]{:S(2)}) copy-start(bf16[2,4,64,256]{3,2,1,0:T(8,128)(2,1)} %param.15) | copy-start | bytes 786436
  7.2 76.8 %all-gather.4.cloned.1.call-start = ((), (), s32[]{:S(2)}) async-start(), calls=%async_computation | async-start | bytes 8650752 | tf_op jit(solution)/shard_map/all_gather | solution.py:30
  8.2 6.8 %collective-permute-start = (bf16[2,1,64,256]{3,2,1,0:T(8,128)(2,1)S(1)}, bf16[2,1,64,256]{3,2,1,0:T(8,128)(2,1)S(1)}, u32[]{:S(2)}, u32[]{:S(2)}) collective-permute-start(bf16[2,1,64,256]{3,2,1,0:T(8,128)(2,1)S(1)} %get-tuple-element.436), channel_id=1, source_target_pairs={{0,1},{1,2},{2,3},{3,4},{4,5},{5,6},{6,7},{8,9},{9,10},{10,11},{11... | collective-permute-start | bytes 196616 | tf_op jit(solution)/shard_map/ppermute | solution.py:19
  12.1 6.2 %collective-permute-start.1 = (bf16[2,1,64,256]{3,2,1,0:T(8,128)(2,1)S(1)}, bf16[2,1,64,256]{3,2,1,0:T(8,128)(2,1)S(1)}, u32[]{:S(2)}, u32[]{:S(2)}) collective-permute-start(bf16[2,1,64,256]{3,2,1,0:T(8,128)(2,1)S(1)} %get-tuple-element.437), channel_id=1, source_target_pairs={{1,0},{2,1},{3,2},{4,3},{5,4},{6,5},{7,6},{9,8},{10,9},{11,10},{12... | collective-permute-start | bytes 196616 | tf_op jit(solution)/shard_map/ppermute | solution.py:21
  20.6 1.5 copy-start.2
  20.6 1.5 copy-start.4
  23.2 157.2 %all-gather.6.cloned.1.call-start = ((), (), s32[]{:S(2)}) async-start(), calls=%async_computation.1 | async-start | bytes 8650752 | tf_op jit(solution)/shard_map/all_gather | solution.py:30
  84.0 37.0 %copy-start.3 = (bf16[256,256]{1,0:T(8,128)(2,1)S(1)}, bf16[256,256]{1,0:T(8,128)(2,1)}, u32[]{:S(2)}) copy-start(bf16[256,256]{1,0:T(8,128)(2,1)} %param.18) | copy-start | bytes 393220
  84.0 37.0 %copy-start.5 = (bf16[2,4,64,256]{3,2,1,0:T(8,128)(2,1)S(1)}, bf16[2,4,64,256]{3,2,1,0:T(8,128)(2,1)}, u32[]{:S(2)}) copy-start(bf16[2,4,64,256]{3,2,1,0:T(8,128)(2,1)} %param.16) | copy-start | bytes 786436
  122.8 378.0 %all-reduce.6.cloned.1.call-start = ((), (), s32[]{:S(2)}) async-start(), calls=%async_computation.2 | async-start | bytes 5242880 | tf_op jit(solution)/shard_map/psum | solution.py:150
  225.1 8.7 %collective-permute-start.2 = (bf16[2,1,64,256]{3,2,1,0:T(8,128)(2,1)S(1)}, bf16[2,1,64,256]{3,2,1,0:T(8,128)(2,1)S(1)}, u32[]{:S(2)}, u32[]{:S(2)}) collective-permute-start(bf16[2,1,64,256]{3,2,1,0:T(8,128)(2,1)S(1)} %get-tuple-element.434), channel_id=1, source_target_pairs={{0,1},{1,2},{2,3},{3,4},{4,5},{5,6},{6,7},{8,9},{9,10},{10,11},{11... | collective-permute-start | bytes 196616 | tf_op jit(solution)/shard_map/ppermute | solution.py:19
  228.6 6.2 %collective-permute-start.3 = (bf16[2,1,64,256]{3,2,1,0:T(8,128)(2,1)S(1)}, bf16[2,1,64,256]{3,2,1,0:T(8,128)(2,1)S(1)}, u32[]{:S(2)}, u32[]{:S(2)}) collective-permute-start(bf16[2,1,64,256]{3,2,1,0:T(8,128)(2,1)S(1)} %get-tuple-element.435), channel_id=1, source_target_pairs={{1,0},{2,1},{3,2},{4,3},{5,4},{6,5},{7,6},{9,8},{10,9},{11,10},{12... | collective-permute-start | bytes 196616 | tf_op jit(solution)/shard_map/ppermute | solution.py:21
  234.9 1.0 copy-start.6
  234.9 0.9 copy-start.7
Sparse Core Ops, SparseCore 0:
  23.3 60.6 all-gather.3
  122.9 57.4 all-gather.5
  233.9 266.8 all-reduce.5
where the time goes:
time: 513 us; the launch traced here: 510 us
  waiting for transfers between devices  350 us (68%)
  other arithmetic  79.8 us (16%)
  blocking collectives  24.2 us (5%)
  local copies, waits for them, and re-layouts  22.5 us (4%)
  between operations  14.2 us (3%)
  starting transfers between devices  9.99 us (2%)
  matrix products  7.92 us (2%)
    psum x1, waiting for transfers between devices, local(): lax.psum((kernel_term, readout_term), ('tm', 'row'))  263 us
    all_gather x2, waiting for transfers between devices, carried_in(): pieces = jax.tree.map(lambda part: lax.all_gather(part, axis), value)  82.3 us
    select_n x62, other arithmetic, turn(): jnp.where(position < mine, new, old)  71.3 us
    all_gather x1, blocking collectives, carried_in(): pieces = jax.tree.map(lambda part: lax.all_gather(part, axis), value)  24.2 us
  transfers between devices with their start and end apart: 7, of which 5 were waited for; matrix products, arithmetic and copies ran while one was open for 4% of the time, Pallas kernels for 0%

commit v1 on v0

--- a/solution.py
+++ b/solution.py
@@ -147,7 +147,7 @@
     band_count = lax.axis_size("row")
     scaling = 1.0 / math.sqrt(cell_count * lax.axis_size("tm") * band_count)
     share_width = channels // band_count
-    kernel_all, readout_all = lax.psum((kernel_term, readout_term), ("tm", "row"))
+    kernel_all, readout_all = lax.psum(lax.psum((kernel_term, readout_term), "row"), "tm")
     offset_start = lax.axis_index("row") * share_width
     kernel_part = lax.dynamic_slice_in_dim(kernel_all, offset_start, share_width, 1)
     readout_part = lax.dynamic_slice_in_dim(readout_all, offset_start, share_width, 1)

time: 513 us -> 448 us (0.87)
  waiting for transfers between devices: 350 us -> 276 us
    psum x1 -> x2, waiting for transfers between devices: 263 us -> 185 us  [the longest x1 113 us: local(): lax.psum(lax.psum((kernel_term, readout_term), 'row'), 'tm')]
  transfers between devices with their start and end apart: 7 -> 8, of which waited for: 5 -> 7; matrix products, arithmetic and copies ran while one was open for 4% -> 5% of each run, Pallas kernels for 0% -> 0%
where the time goes in v1:
time: 448 us; the launch traced here: 444 us
  waiting for transfers between devices  276 us (62%)
  other arithmetic  82 us (18%)
  local copies, waits for them, and re-layouts  26.3 us (6%)
  blocking collectives  24.2 us (5%)
  between operations  14.1 us (3%)
  starting transfers between devices  10 us (2%)
  matrix products  9.57 us (2%)
    psum x1, waiting for transfers between devices, local(): lax.psum(lax.psum((kernel_term, readout_term), 'row'), 'tm')  113 us
    all_gather x2, waiting for transfers between devices, carried_in(): pieces = jax.tree.map(lambda part: lax.all_gather(part, axis), value)  82.3 us
    psum x1, waiting for transfers between devices, local(): lax.psum((kernel_term, readout_term), 'row')  72.8 us
    select_n x62, other arithmetic, turn(): jnp.where(position < mine, new, old)  71.3 us
    all_gather x1, blocking collectives, carried_in(): pieces = jax.tree.map(lambda part: lax.all_gather(part, axis), value)  24.2 us
  transfers between devices with their start and end apart: 8, of which 7 were waited for; matrix products, arithmetic and copies ran while one was open for 5% of the time, Pallas kernels for 0%

profile of v1, /device:TPU:2, one launch (start us, length us, event | category | flops | bytes accessed | tf_op | source)
XLA Modules:
  0.0 444.0 jit_solution(8415605560546625735)
XLA Ops:
  8.2 3.8 collective-permute-start
  12.1 1.3 collective-permute-start.1
  15.1 3.2 collective-permute-done.1
  23.3 24.2 %all-gather = f32[32,1,256]{2,1,0:T(1,128)S(1)} all-gather(f32[1,1,256]{2,1,0:T(1,128)S(1)} %slice_bitcast_fusion.12), channel_id=1, replica_groups=mesh['tm'=32,'row'=8] {'tm'}, dimensions={0}, use_global_device_ids=true | all-gather | bytes 33792 | tf_op jit(solution)/shard_map/all_gather | solution.py:30
  47.6 36.4 %all-gather.4.cloned.1.call-done = f32[32,4,64,256]{3,2,1,0:T(8,128)} async-done(((f32[1,4,64,256]{3,2,1,0:T(8,128)}), f32[32,4,64,256]{3,2,1,0:T(8,128)}) %all-gather.4.cloned.1.call-update) | async-done | bytes 8388624 | tf_op jit(solution)/shard_map/all_gather | solution.py:30
  84.0 36.9 %while.58 = (s32[]{:T(128)}, f32[4,64,256]{2,1,0:T(8,128)S(1)}, s32[]{:T(128)}, f32[32,256]{1,0:T(8,128)S(1)}, f32[32,4,64,256]{3,2,1,0:T(8,128)}, /*index=5*/s32[]{:T(128)}, s32[]{:T(128)}) while((s32[]{:T(128)}, f32[4,64,256]{2,1,0:T(8,128)S(1)}, s32[]{:T(128)}, f32[32,256]{1,0:T(8,128)S(1)}, f32[32,4,64,256]{3,2,1,0:T(8,128)}, ...), condition=%wide.region_4.5_spmd.clone, body=%wide.region_3.4_spmd.clone.sunk | while | flops 262148 | bytes 789609 | solution.py:42
  84.0 1.2 fusion.59
  85.2 1.1 fusion.59
  86.4 1.1 fusion.59
  123.2 3.3 copy.51
  126.5 2.8 copy.57
  129.3 4.3 copy.52
  134.6 45.9 %all-gather.6.cloned.1.call-done = f32[32,4,64,256]{3,2,1,0:T(8,128)} async-done(((f32[1,4,64,256]{3,2,1,0:T(8,128)}), f32[32,4,64,256]{3,2,1,0:T(8,128)}) %all-gather.6.cloned.1.call-update) | async-done | bytes 8388624 | tf_op jit(solution)/shard_map/all_gather | solution.py:30
  180.4 7.7 %rev.16 = f32[32,4,64,256]{3,2,1,0:T(8,128)} reverse(f32[32,4,64,256]{3,2,1,0:T(8,128)} %all-gather.6.cloned.1.call-done), dimensions={0} | reverse | bytes 16777216 | tf_op jit(solution)/shard_map/rev | solution.py:32
  188.2 36.8 %while.60 = (s32[]{:T(128)}, f32[4,64,256]{2,1,0:T(8,128)S(1)}, s32[]{:T(128)}, f32[32,256]{1,0:T(8,128)S(1)}, f32[32,4,64,256]{3,2,1,0:T(8,128)}, /*index=5*/s32[]{:T(128)}, s32[]{:T(128)}) while((s32[]{:T(128)}, f32[4,64,256]{2,1,0:T(8,128)S(1)}, s32[]{:T(128)}, f32[32,256]{1,0:T(8,128)S(1)}, f32[32,4,64,256]{3,2,1,0:T(8,128)}, ...), condition=%wide.region_9.10_spmd.clone, body=%wide.region_8.9_spmd.clone.sunk | while | flops 262148 | bytes 789609 | solution.py:42
  225.1 3.9 fusion.45
  229.1 3.5 collective-permute-start.2
  232.5 1.3 collective-permute-start.3
  234.4 4.3 collective-permute-done.3
  241.9 72.8 %all-reduce.10.cloned.1.call-done = (f32[9,256,256]{2,1,0:T(8,128)}, f32[256,256]{0,1:T(8,128)}) async-done(((f32[9,256,256]{2,1,0:T(8,128)}, f32[256,256]{0,1:T(8,128)}), (f32[9,256,256]{2,1,0:T(8,128)}, f32[256,256]{0,1:T(8,128)})) %all-reduce.10.cloned.1.call-update) | async-done | bytes 2621456 | tf_op jit(solution)/shard_map/psum | solution.py:150
  318.5 3.2 fusion.4
  321.7 112.7 %all-reduce.8.cloned.1.call-done = (f32[9,256,256]{2,1,0:T(8,128)}, f32[256,256]{0,1:T(8,128)}) async-done(((f32[9,256,256]{2,1,0:T(8,128)}, f32[256,256]{0,1:T(8,128)}), (f32[9,256,256]{2,1,0:T(8,128)}, f32[256,256]{0,1:T(8,128)})) %all-reduce.8.cloned.1.call-update) | async-done | bytes 2621456 | tf_op jit(solution)/shard_map/psum | solution.py:150
  434.4 1.7 dynamic-slice_multiply_fusion
  436.1 1.4 dynamic-slice_multiply_fusion.1
  (203 shorter events, 87.5 us)
Async XLA Ops:
  7.2 13.5 %copy-start = (bf16[9,256,256]{2,1,0:T(8,128)(2,1)S(1)}, bf16[9,256,256]{2,1,0:T(8,128)(2,1)}, u32[]{:S(2)}) copy-start(bf16[9,256,256]{2,1,0:T(8,128)(2,1)} %param.17) | copy-start | bytes 3538948
  7.2 13.2 %copy-start.1 = (bf16[2,4,64,256]{3,2,1,0:T(8,128)(2,1)S(1)}, bf16[2,4,64,256]{3,2,1,0:T(8,128)(2,1)}, u32[]{:S(2)}) copy-start(bf16[2,4,64,256]{3,2,1,0:T(8,128)(2,1)} %param.15) | copy-start | bytes 786436
  7.2 76.8 %all-gather.4.cloned.1.call-start = ((), (), s32[]{:S(2)}) async-start(), calls=%async_computation | async-start | bytes 8650752 | tf_op jit(solution)/shard_map/all_gather | solution.py:30
  8.2 6.8 %collective-permute-start = (bf16[2,1,64,256]{3,2,1,0:T(8,128)(2,1)S(1)}, bf16[2,1,64,256]{3,2,1,0:T(8,128)(2,1)S(1)}, u32[]{:S(2)}, u32[]{:S(2)}) collective-permute-start(bf16[2,1,64,256]{3,2,1,0:T(8,128)(2,1)S(1)} %get-tuple-element.438), channel_id=1, source_target_pairs={{0,1},{1,2},{2,3},{3,4},{4,5},{5,6},{6,7},{8,9},{9,10},{10,11},{11... | collective-permute-start | bytes 196616 | tf_op jit(solution)/shard_map/ppermute | solution.py:19
  12.1 6.2 %collective-permute-start.1 = (bf16[2,1,64,256]{3,2,1,0:T(8,128)(2,1)S(1)}, bf16[2,1,64,256]{3,2,1,0:T(8,128)(2,1)S(1)}, u32[]{:S(2)}, u32[]{:S(2)}) collective-permute-start(bf16[2,1,64,256]{3,2,1,0:T(8,128)(2,1)S(1)} %get-tuple-element.439), channel_id=1, source_target_pairs={{1,0},{2,1},{3,2},{4,3},{5,4},{6,5},{7,6},{9,8},{10,9},{11,10},{12... | collective-permute-start | bytes 196616 | tf_op jit(solution)/shard_map/ppermute | solution.py:21
  20.6 1.5 copy-start.2
  20.6 1.5 copy-start.4
  23.2 157.2 %all-gather.6.cloned.1.call-start = ((), (), s32[]{:S(2)}) async-start(), calls=%async_computation.1 | async-start | bytes 8650752 | tf_op jit(solution)/shard_map/all_gather | solution.py:30
  84.0 37.0 %copy-start.3 = (bf16[256,256]{1,0:T(8,128)(2,1)S(1)}, bf16[256,256]{1,0:T(8,128)(2,1)}, u32[]{:S(2)}) copy-start(bf16[256,256]{1,0:T(8,128)(2,1)} %param.18) | copy-start | bytes 393220
  84.0 37.0 %copy-start.5 = (bf16[2,4,64,256]{3,2,1,0:T(8,128)(2,1)S(1)}, bf16[2,4,64,256]{3,2,1,0:T(8,128)(2,1)}, u32[]{:S(2)}) copy-start(bf16[2,4,64,256]{3,2,1,0:T(8,128)(2,1)} %param.16) | copy-start | bytes 786436
  122.8 191.8 %all-reduce.10.cloned.1.call-start = ((), (), s32[]{:S(2)}) async-start(), calls=%async_computation.3 | async-start | bytes 5242880 | tf_op jit(solution)/shard_map/psum | solution.py:150
  229.0 205.4 %all-reduce.8.cloned.1.call-start = ((), (), s32[]{:S(2)}) async-start(), calls=%async_computation.2 | async-start | bytes 5242880 | tf_op jit(solution)/shard_map/psum | solution.py:150
  229.1 5.3 %collective-permute-start.2 = (bf16[2,1,64,256]{3,2,1,0:T(8,128)(2,1)S(1)}, bf16[2,1,64,256]{3,2,1,0:T(8,128)(2,1)S(1)}, u32[]{:S(2)}, u32[]{:S(2)}) collective-permute-start(bf16[2,1,64,256]{3,2,1,0:T(8,128)(2,1)S(1)} %get-tuple-element.436), channel_id=1, source_target_pairs={{0,1},{1,2},{2,3},{3,4},{4,5},{5,6},{6,7},{8,9},{9,10},{10,11},{11... | collective-permute-start | bytes 196616 | tf_op jit(solution)/shard_map/ppermute | solution.py:19
  232.5 6.2 %collective-permute-start.3 = (bf16[2,1,64,256]{3,2,1,0:T(8,128)(2,1)S(1)}, bf16[2,1,64,256]{3,2,1,0:T(8,128)(2,1)S(1)}, u32[]{:S(2)}, u32[]{:S(2)}) collective-permute-start(bf16[2,1,64,256]{3,2,1,0:T(8,128)(2,1)S(1)} %get-tuple-element.437), channel_id=1, source_target_pairs={{1,0},{2,1},{3,2},{4,3},{5,4},{6,5},{7,6},{9,8},{10,9},{11,10},{12... | collective-permute-start | bytes 196616 | tf_op jit(solution)/shard_map/ppermute | solution.py:21
  314.7 3.9 copy-start.6
  314.7 3.9 copy-start.7
Sparse Core Ops, SparseCore 0:
  23.3 60.6 all-gather.3
  123.0 57.4 all-gather.5
  229.1 85.5 all-reduce.9
  317.9 116.4 all-reduce.7
